TPU v7x, 32 devices: a whole 2x2x4 slice. The times are simulated.
32 devices in a mesh: groups: 2 (over x), modes: 16 (over z, y, core).
Axes of the slice: x: 2, y: 2, z: 4, core: 2. Of those that a mesh axis runs over, the one named last changes fastest.
Arguments:
- mode_fields: bfloat16 [256, 256, 2048], P(('groups', 'modes')), parts along dimension 0, may hold values from -0.59765625 to 0.59765625
- coeff: float32 [256], P('groups'), parts along dimension 0, may hold values from -6 to 6
- eigen: float32 [256], P('groups'), parts along dimension 0, may hold values from 0.1 to 100
- map_friction: float32 [512, 2048], P(('groups', 'modes')), parts along dimension 0, may hold values from 1 to 2.5
- bed: float32 [512, 2048], P(('groups', 'modes')), parts along dimension 0, may hold values from -5 to 5
- smb: float32 [512, 2048], P(('groups', 'modes')), parts along dimension 0, may hold values from -0.6 to 0.4
- thickness: float32 [512, 2048], P(('groups', 'modes')), parts along dimension 0, may hold values from 1.9 to 2.6
Outputs:
- log_friction: float32 [512, 2048], P(('groups', 'modes')), parts along dimension 0
- final_thickness: float32 [512, 2048], P(('groups', 'modes')), parts along dimension 0
There are 2 independent parts, one for each index of `groups`. A program takes and returns all parts, laid end to end along the dimension named above; each array names one. Nothing has to cross between parts.
All inputs are finite; a program needn't handle non-finite values.
Results may differ from a plain program's by a relative error of at most 0.0014.
Values may be sent and summed in bfloat16 or wider, within the bound.
A program may use at most 64 MiB of HBM per device.

v0:
```python
import jax
import jax.numpy as jnp
from jax import lax
from jax.sharding import PartitionSpec as P

STEPS = 8


flow_rate = 0.02
slide_rate = 0.1
diff_cap = 0.5
time_step = 0.4


def padded(value, sides, width):
    for axis, dim in sides:
        peers, length = (lax.axis_size(axis), value.shape[dim])
        up = [(i, (i + 1) % peers) for i in range(peers - 1)]
        down = [(j, i) for i, j in up]
        last = lax.slice_in_dim(value, length - width, length, axis=dim)
        leading = lax.slice_in_dim(value, 0, width, axis=dim)
        before = lax.ppermute(last, axis, up)
        after = lax.ppermute(leading, axis, down)
        value = jnp.concatenate([before, value, after], axis=dim)
    return value


def advance(height, base, friction, balance):
    hpad = jnp.pad(height, ((0, 0), (2, 2)))
    bpad = jnp.pad(base, ((0, 0), (2, 2)))
    fpad = jnp.pad(friction, ((0, 0), (2, 2)))
    surface = bpad + hpad
    grad_x = (surface[2:, 1:-1] - surface[:-2, 1:-1]) * 0.5
    grad_y = (surface[1:-1, 2:] - surface[1:-1, :-2]) * 0.5
    center = hpad[1:-1, 1:-1]
    fcent = fpad[1:-1, 1:-1]
    squared = center * center
    diff = flow_rate * squared * squared * center * (grad_x * grad_x + grad_y * grad_y)
    diff = jnp.minimum(diff + slide_rate * squared * jnp.exp(-fcent), diff_cap)
    scent = surface[1:-1, 1:-1]
    mid_d = diff[1:-1, 1:-1]
    mid_s = scent[1:-1, 1:-1]
    up_x = 0.5 * (diff[2:, 1:-1] + mid_d) * (scent[2:, 1:-1] - mid_s)
    down_x = 0.5 * (mid_d + diff[:-2, 1:-1]) * (mid_s - scent[:-2, 1:-1])
    up_y = 0.5 * (diff[1:-1, 2:] + mid_d) * (scent[1:-1, 2:] - mid_s)
    down_y = 0.5 * (mid_d + diff[1:-1, :-2]) * (mid_s - scent[1:-1, :-2])
    total = up_x - down_x + up_y - down_y
    return jnp.maximum(height[2:-2] + time_step * (total + balance[2:-2]), 0.0)


def march(extended, count, wide, reach, first, total_rows):
    for inner_step in range(count):
        begin = reach - 2 * count + 2 * inner_step
        length = extended.shape[0]
        statics = wide[:, begin : begin + length]
        extended = advance(extended, statics[0], statics[1], statics[2])
        remain = 2 * count - 2 * inner_step - 2
        if remain > 0:
            global_row = first - remain + jnp.arange(extended.shape[0], dtype=jnp.int32)
            inside = (global_row >= 0) & (global_row < total_rows)
            extended = jnp.where(inside[:, None], extended, 0.0)
    return extended


def per_device(mode_fields, coeff, eigen, map_friction, bed, smb, thickness):
    weights = (coeff / jnp.sqrt(1.0 + eigen)).astype(jnp.bfloat16)
    rows_dev = map_friction.shape[0]
    mode_dev = mode_fields.shape[0]
    local_w = lax.dynamic_slice_in_dim(weights, lax.axis_index("modes") * mode_dev, mode_dev, 0)
    perturb = lax.psum_scatter(
        jnp.einsum("k,kxy->xy", local_w, mode_fields, preferred_element_type=jnp.float32),
        "modes",
        scatter_dimension=0,
        tiled=True,
    )
    log_friction = map_friction + perturb
    per_round = min(STEPS, rows_dev // 2)
    reach = 2 * per_round
    statics = jnp.stack([bed, log_friction, smb])
    wide = padded(statics, (("modes", 1),), reach)
    first = lax.axis_index("modes") * rows_dev
    total_rows = rows_dev * lax.axis_size("modes")
    height = thickness
    extended = padded(height, (("modes", 0),), 2 * per_round)
    height = march(extended, per_round, wide, reach, first, total_rows)
    return (log_friction, height)


def solution(mesh):
    return jax.shard_map(
        per_device,
        mesh=mesh,
        in_specs=(
            P(("groups", "modes"), None, None),
            P("groups"),
            P("groups"),
            P(("groups", "modes"), None),
            P(("groups", "modes"), None),
            P(("groups", "modes"), None),
            P(("groups", "modes"), None),
        ),
        out_specs=(P(("groups", "modes"), None), P(("groups", "modes"), None)),
        check_vma=False,
    )
```

profile of v0, /device:TPU:5, one launch (start us, length us, event | category | flops | bytes accessed | tf_op | source)
XLA Modules:
  0.0 117.0 jit_solution(11758352358127257634)
XLA Ops:
  7.2 0.0 reduce-scatter.2.cloned.1.call-start
  7.2 0.7 multiply_convert_fusion
  7.9 9.4 %fusion = f32[1,256,2048]{2,0,1:T(1,128)S(1)} fusion(bf16[8,256,2048]{2,1,0:T(8,128)(2,1)} %param.7, bf16[128]{0:T(256)(128)(2,1)S(1)} %multiply_convert_fusion, s32[]{:T(128)S(6)} %select_n.31), kind=kOutput, calls=%fused_computation | convolution fusion | flops 8388608 | bytes 10486020 | tf_op jit(solution)/shard_map/k,kxy->xy/dot_general | solution.py:71
  17.3 2.2 %copy.14 = f32[1,256,2048]{2,1,0:T(8,128)} copy(f32[1,256,2048]{2,0,1:T(1,128)S(1)} %fusion) | data formatting | bytes 4194304 | tf_op jit(solution)/shard_map/k,kxy->xy/dot_general | solution.py:71
  19.5 0.0 copy-start.4
  19.5 0.0 copy-start.3
  19.5 0.0 copy-start.1
  19.5 0.0 copy-start.2
  19.5 0.0 reduce-scatter.2.cloned.1.call-update
  19.5 0.9 copy-done.4
  20.4 3.7 %collective-permute-start = (f32[16,2048]{1,0:T(8,128)S(1)}, f32[16,2048]{1,0:T(8,128)S(1)}, u32[]{:S(2)}, u32[]{:S(2)}) collective-permute-start(f32[16,2048]{1,0:T(8,128)S(1)} %copy-done.4), channel_id=1, source_target_pairs={{0,1},{1,2},{2,3},{3,4},{4,5},{5,6},{6,7},{7,8},{8,9},{9,10},{10,1... | collective-permute-start | bytes 393224 | tf_op jit(solution)/shard_map/ppermute | solution.py:22
  24.1 1.9 %collective-permute-start.1 = (f32[16,2048]{1,0:T(8,128)S(1)}, f32[16,2048]{1,0:T(8,128)S(1)}, u32[]{:S(2)}, u32[]{:S(2)}) collective-permute-start(f32[16,2048]{1,0:T(8,128)S(1)} %copy-done.4), channel_id=1, source_target_pairs={{1,0},{2,1},{3,2},{4,3},{5,4},{6,5},{7,6},{8,7},{9,8},{10,9},{11,1... | collective-permute-start | bytes 393224 | tf_op jit(solution)/shard_map/ppermute | solution.py:23
  26.1 0.0 collective-permute-done
  26.2 54.2 %reduce-scatter.2.cloned.1.call-done = f32[16,2048]{1,0:T(8,128)} async-done(((f32[256,2048]{1,0:T(8,128)}), f32[16,2048]{1,0:T(8,128)}) %reduce-scatter.2.cloned.1.call-update) | async-done | bytes 131088 | tf_op jit(solution)/shard_map/reduce_scatter | solution.py:70
  80.4 0.0 copy-done.3
  80.4 0.9 add.382
  81.3 0.0 copy-start
  81.4 0.0 copy-done.1
  81.4 0.0 copy-done.2
  81.4 5.8 %collective-permute-start.2 = (f32[3,16,2048]{2,1,0:T(8,128)S(1)}, f32[3,16,2048]{2,1,0:T(8,128)S(1)}, u32[]{:S(2)}, u32[]{:S(2)}) collective-permute-start(f32[3,16,2048]{2,1,0:T(8,128)S(1)} %pad_maximum_fusion.1), channel_id=1, source_target_pairs={{0,1},{1,2},{2,3},{3,4},{4,5},{5,6},{6,7},{7,8},{8,9},{9,10},{10,1... | collective-permute-start | bytes 1179656 | tf_op jit(solution)/shard_map/ppermute | solution.py:22
  87.2 2.1 %collective-permute-start.3 = (f32[3,16,2048]{2,1,0:T(8,128)S(1)}, f32[3,16,2048]{2,1,0:T(8,128)S(1)}, u32[]{:S(2)}, u32[]{:S(2)}) collective-permute-start(f32[3,16,2048]{2,1,0:T(8,128)S(1)} %pad_maximum_fusion.1), channel_id=1, source_target_pairs={{1,0},{2,1},{3,2},{4,3},{5,4},{6,5},{7,6},{8,7},{9,8},{10,9},{11,1... | collective-permute-start | bytes 1179656 | tf_op jit(solution)/shard_map/ppermute | solution.py:23
  89.3 0.0 collective-permute-done.1
  89.3 2.5 %collective-permute-done.2 = f32[3,16,2048]{2,1,0:T(8,128)S(1)} collective-permute-done((f32[3,16,2048]{2,1,0:T(8,128)S(1)}, f32[3,16,2048]{2,1,0:T(8,128)S(1)}, u32[]{:S(2)}, u32[]{:S(2)}) %collective-permute-start.2) | collective-permute-done | bytes 393248 | tf_op jit(solution)/shard_map/ppermute | solution.py:22
  91.9 5.3 %collective-permute-done.3 = f32[3,16,2048]{2,1,0:T(8,128)S(1)} collective-permute-done((f32[3,16,2048]{2,1,0:T(8,128)S(1)}, f32[3,16,2048]{2,1,0:T(8,128)S(1)}, u32[]{:S(2)}, u32[]{:S(2)}) %collective-permute-start.3) | collective-permute-done | bytes 393248 | tf_op jit(solution)/shard_map/ppermute | solution.py:23
  97.2 0.1 pad_maximum_fusion
  97.3 0.0 copy-done
  97.3 0.1 slice_bitcast_fusion.3
  97.3 0.1 slice_bitcast_fusion
  97.4 0.1 slice_bitcast_fusion.8
  97.5 0.1 slice_bitcast_fusion.5
  97.7 0.9 fusion.5
  98.6 1.2 %fusion.24 = f32[44,2048]{1,0:T(8,128)S(1)} fusion(f32[3,48,2048]{2,1,0:T(8,128)S(1)} %pad_maximum_fusion, f32[48,2048]{1,0:T(8,128)S(1)} %constant_dynamic-update-slice_fusion, f32[48,2048]{1,0:T(8,128)S(1)} %get-tuple-element.17, f32[46,2050]{1,0:T(8,128)S(1)} %fusion.5, pred[44]{0:T(512)(128)(4,1)S(1)} %compare_and_fusion), kind=kLoop, calls=%fused_computation.39 | loop fusion | flops 2613248 | bytes 3899904 | tf_op jit(solution)/shard_map/jit(_where)/select_n | solution.py:61
  99.9 0.9 fusion.9
  100.8 1.0 fusion.67
  101.8 0.8 fusion.43
  102.6 0.9 fusion.80
  103.5 0.8 fusion.47
  104.3 0.7 fusion.129
  105.0 0.7 fusion.105
  105.7 0.7 fusion.142
  106.4 0.6 fusion.109
  107.1 0.5 fusion.191
  107.6 0.5 fusion.167
  108.1 0.5 fusion.204
  108.6 0.5 fusion.171
  109.2 1.0 fusion.234
  (15 shorter events, 0.3 us)
Async XLA Ops:
  7.2 73.3 %reduce-scatter.2.cloned.1.call-start = ((), (), s32[]{:S(2)}) async-start(), calls=%async_computation.1 | async-start | bytes 2228224 | tf_op jit(solution)/shard_map/reduce_scatter | solution.py:70
  19.5 0.9 copy-start.4
  19.5 60.9 %copy-start.3 = (f32[16,2048]{1,0:T(8,128)S(1)}, f32[16,2048]{1,0:T(8,128)}, u32[]{:S(2)}) copy-start(f32[16,2048]{1,0:T(8,128)} %param.10) | copy-start | bytes 393220
  19.5 61.9 %copy-start.1 = (f32[16,2048]{1,0:T(8,128)S(1)}, f32[16,2048]{1,0:T(8,128)}, u32[]{:S(2)}) copy-start(f32[16,2048]{1,0:T(8,128)} %param.12) | copy-start | bytes 393220
  19.5 61.9 %copy-start.2 = (f32[16,2048]{1,0:T(8,128)S(1)}, f32[16,2048]{1,0:T(8,128)}, u32[]{:S(2)}) copy-start(f32[16,2048]{1,0:T(8,128)} %param.11) | copy-start | bytes 393220
  20.4 5.8 %collective-permute-start = (f32[16,2048]{1,0:T(8,128)S(1)}, f32[16,2048]{1,0:T(8,128)S(1)}, u32[]{:S(2)}, u32[]{:S(2)}) collective-permute-start(f32[16,2048]{1,0:T(8,128)S(1)} %copy-done.4), channel_id=1, source_target_pairs={{0,1},{1,2},{2,3},{3,4},{4,5},{5,6},{6,7},{7,8},{8,9},{9,10},{10,1... | collective-permute-start | bytes 393224 | tf_op jit(solution)/shard_map/ppermute | solution.py:22
  24.1 65.2 %collective-permute-start.1 = (f32[16,2048]{1,0:T(8,128)S(1)}, f32[16,2048]{1,0:T(8,128)S(1)}, u32[]{:S(2)}, u32[]{:S(2)}) collective-permute-start(f32[16,2048]{1,0:T(8,128)S(1)} %copy-done.4), channel_id=1, source_target_pairs={{1,0},{2,1},{3,2},{4,3},{5,4},{6,5},{7,6},{8,7},{9,8},{10,9},{11,1... | collective-permute-start | bytes 393224 | tf_op jit(solution)/shard_map/ppermute | solution.py:23
  81.3 15.9 %copy-start = (f32[16,2048]{1,0:T(8,128)}, f32[16,2048]{1,0:T(8,128)S(1)}, u32[]{:S(2)}) copy-start(f32[16,2048]{1,0:T(8,128)S(1)} %add.382) | copy-start | bytes 393220
  81.4 10.5 %collective-permute-start.2 = (f32[3,16,2048]{2,1,0:T(8,128)S(1)}, f32[3,16,2048]{2,1,0:T(8,128)S(1)}, u32[]{:S(2)}, u32[]{:S(2)}) collective-permute-start(f32[3,16,2048]{2,1,0:T(8,128)S(1)} %pad_maximum_fusion.1), channel_id=1, source_target_pairs={{0,1},{1,2},{2,3},{3,4},{4,5},{5,6},{6,7},{7,8},{8,9},{9,10},{10,1... | collective-permute-start | bytes 1179656 | tf_op jit(solution)/shard_map/ppermute | solution.py:22
  87.2 10.0 %collective-permute-start.3 = (f32[3,16,2048]{2,1,0:T(8,128)S(1)}, f32[3,16,2048]{2,1,0:T(8,128)S(1)}, u32[]{:S(2)}, u32[]{:S(2)}) collective-permute-start(f32[3,16,2048]{2,1,0:T(8,128)S(1)} %pad_maximum_fusion.1), channel_id=1, source_target_pairs={{1,0},{2,1},{3,2},{4,3},{5,4},{6,5},{7,6},{8,7},{9,8},{10,9},{11,1... | collective-permute-start | bytes 1179656 | tf_op jit(solution)/shard_map/ppermute | solution.py:23
Sparse Core Ops, SparseCore 0:
  19.6 60.7 reduce-scatter.1
where the time goes:
time: 118 us; the launch traced here: 117 us
  waiting for transfers between devices  62.1 us (53%)
  between operations  14.4 us (12%)
  other arithmetic  14.2 us (12%)
  starting transfers between devices  13.5 us (11%)
  matrix products  9.37 us (8%)
  local copies, waits for them, and re-layouts  3.52 us (3%)
    reduce_scatter x1, waiting for transfers between devices, per_device(): lax.psum_scatter(jnp.einsum('k,kxy->xy', local_w, mode_fields, preferred_...  54.2 us
    ppermute x2, starting transfers between devices, padded(): before = lax.ppermute(last, axis, up)  9.45 us
    dot_general x1, matrix products, per_device(): jnp.einsum('k,kxy->xy', local_w, mode_fields, preferred_element_type=jnp....  9.37 us
    min x8, other arithmetic, advance(): diff = jnp.minimum(diff + slide_rate * squared * jnp.exp(-fcent), diff_cap)  5.76 us
    select_n x7, other arithmetic, march(): extended = jnp.where(inside[:, None], extended, 0.0)  5.59 us
    ppermute x2, waiting for transfers between devices, padded(): after = lax.ppermute(leading, axis, down)  5.3 us
    ppermute x2, starting transfers between devices, padded(): after = lax.ppermute(leading, axis, down)  4.02 us
    ppermute x2, waiting for transfers between devices, padded(): before = lax.ppermute(last, axis, up)  2.54 us
  transfers between devices with their start and end apart: 5, of which 3 were waited for; matrix products, arithmetic and copies ran while one was open for 1% of the time, Pallas kernels for 0%

commit v1 on v0

v1 whole, which is shorter than its diff:
```python
import functools

import jax
import jax.numpy as jnp
from jax import lax
from jax.experimental import pallas as pl
from jax.experimental.pallas import tpu as pltpu
from jax.sharding import PartitionSpec as P

STEPS = 8

flow_rate = 0.02
slide_rate = 0.1
diff_cap = 0.5
time_step = 0.4

WIRE = jnp.bfloat16
PAD = 8
F32 = jnp.float32


def kernel(
    n,
    coeff_ref, eigen_ref, map_ref, bed_ref, smb_ref, h0_ref, fields_ref,
    logf_ref, final_ref,
    mf, p1out, p1own, p1in, s2out, s2in, s3out, s3in, acc,
    st_out, st_in, h_in, f_out, f_in,
    ext_b, ext_e, ext_m, ext_h, ext_d, ext_s0, ext_s1,
    mf_sem, p1s, p1r, s2s, s2r, s3s, s3r, hs, hr,
):
    me = lax.axis_index("modes")
    c = me % 2
    a = (me // 2) % 2
    b = me // 4
    B = n // 4
    mode_dev = fields_ref.shape[0]
    rows, cols = map_ref.shape
    ks = list(range(1, B)) + [0]

    def bk(k):
        return lax.rem(b + k, B)

    def dest(k, aa, cc):
        return (bk(k) * 2 + aa) * 2 + cc

    order = [(k, aa, cc) for aa in (1, 0) for k in ks for cc in (1, 0)]

    def dest_of(k, aa, cc):
        return dest(k, a + aa - 2 * a * aa, c + cc - 2 * c * cc)

    def load(i):
        k, aa, cc = order[i]
        rr = pl.ds(pl.multiple_of(dest_of(k, aa, cc) * rows, rows), rows)
        return pltpu.make_async_copy(fields_ref.at[:, rr, :], mf.at[:, pl.ds(i * rows, rows), :], mf_sem.at[i])

    for i in range(n):
        load(i).start()

    left, right = lax.rem(me + n - 1, n), lax.rem(me + 1, n)
    core_peer = me + 1 - 2 * c
    y_peer = me + 2 - 4 * a
    barrier = pltpu.get_barrier_semaphore()

    def z_peer(k):
        return dest(k, a, c)

    for peer in [left, right, core_peer, y_peer] + [z_peer(k) for k in range(1, B)]:
        pl.semaphore_signal(barrier, inc=1, device_id={"modes": peer}, device_id_type=pl.DeviceIdType.MESH)

    w = coeff_ref[...] / jnp.sqrt(1.0 + eigen_ref[...])
    w = w.astype(jnp.bfloat16).astype(F32)
    lane = lax.broadcasted_iota(jnp.int32, w.shape, 1)
    ws = []
    for j in range(mode_dev):
        picked = jnp.where(lane == me * mode_dev + j, w, 0.0)
        ws.append(jnp.sum(picked, axis=1, keepdims=True))
    st_out[0] = bed_ref[...].astype(jnp.bfloat16)
    st_out[1] = smb_ref[...].astype(jnp.bfloat16)

    pl.semaphore_wait(barrier, 4 + B - 1)

    def remote(src, dst, ssem, rsem, peer):
        return pltpu.make_async_remote_copy(
            src_ref=src, dst_ref=dst, send_sem=ssem, recv_sem=rsem,
            device_id={"modes": peer}, device_id_type=pl.DeviceIdType.MESH)

    def halo(kind, side):
        src = (st_out, h0_ref, f_out)[kind]
        dst = (st_in, h_in, f_in)[kind]
        peer = right if side == 0 else left
        at = kind * 2 + side
        return remote(src, dst.at[side], hs.at[at], hr.at[at], peer)

    has_up, has_down = me > 0, me < n - 1

    def start_halo(kind):
        @pl.when(has_down)
        def _():
            halo(kind, 0).start()

        @pl.when(has_up)
        def _():
            halo(kind, 1).start()

    def wait_halo(kind):
        @pl.when(has_down)
        def _():
            halo(kind, 0).wait_send()
            halo(kind, 1).wait_recv()

        @pl.when(has_up)
        def _():
            halo(kind, 1).wait_send()
            halo(kind, 0).wait_recv()

    start_halo(1)
    start_halo(0)

    CT = min(512, cols)

    def col_loop(body):
        def step(j, carry):
            body(pl.ds(pl.multiple_of(j * CT, CT), CT))
            return carry
        lax.fori_loop(0, cols // CT, step, 0)

    def partial(i, out):
        load(i).wait()

        def body(cs):
            tot = None
            for j in range(mode_dev):
                term = mf[j, pl.ds(i * rows, rows), cs].astype(F32) * ws[j]
                tot = term if tot is None else tot + term
            out[:, cs] = tot
        col_loop(body)

    def s1copy(m):
        return remote(p1out.at[m], p1in.at[m], p1s.at[m], p1r.at[m], core_peer)

    def stage1(m):
        partial(2 * m, p1out.at[m])
        s1copy(m).start()
        partial(2 * m + 1, p1own.at[m])

    def s2copy(q):
        return remote(s2out.at[q], s2in.at[q], s2s.at[q], s2r.at[q], y_peer)

    def stage2(q):
        s1copy(q).wait_recv()

        def body(cs):
            s2out[q, :, cs] = (p1own[q, :, cs] + p1in[q, :, cs]).astype(WIRE)
        col_loop(body)
        s2copy(q).start()

    def s3copy(q):
        return remote(s3out.at[q], s3in.at[q], s3s.at[q], s3r.at[q], z_peer(ks[q]))

    def stage3(q):
        m = B + q
        s1copy(m).wait_recv()
        s2copy(q).wait_recv()

        def body(cs):
            tot = p1own[m, :, cs] + p1in[m, :, cs] + s2in[q, :, cs].astype(F32)
            if ks[q]:
                s3out[q, :, cs] = tot.astype(WIRE)
            else:
                acc[:, cs] = tot + map_ref[:, cs]
        col_loop(body)
        if ks[q]:
            s3copy(q).start()

    for q in range(B):
        stage1(q)
        if q:
            stage2(q - 1)
    stage1(B)
    stage2(B - 1)
    for q in range(1, B):
        stage1(B + q)
    for q in range(B):
        stage3(q)
    for q in range(B - 1):
        s3copy(q).wait_recv()

    def finish(cs):
        tot = acc[:, cs]
        for q in range(B - 1):
            tot = tot + s3in[q, :, cs].astype(F32)
        logf_ref[:, cs] = tot
        f_out[:, cs] = tot.astype(jnp.bfloat16)
    col_loop(finish)
    start_halo(2)

    top, mid, low = pl.ds(PAD, rows), pl.ds(PAD + rows, rows), pl.ds(PAD + 2 * rows, rows)
    zeros = jnp.zeros((rows, cols), F32)
    for ref in (ext_s0, ext_s1, ext_d, ext_h):
        ref[pl.ds(0, PAD), :] = jnp.zeros((PAD, cols), F32)
        ref[pl.ds(PAD + 3 * rows, PAD), :] = jnp.zeros((PAD, cols), F32)

    ext_b[mid, :] = bed_ref[...]
    ext_m[mid, :] = time_step * smb_ref[...]
    ext_h[mid, :] = h0_ref[...]
    ext_s0[mid, :] = bed_ref[...] + h0_ref[...]
    ext_e[mid, :] = slide_rate * jnp.exp(-logf_ref[...])
    wait_halo(0)
    wait_halo(1)

    def fill(side, where, present):
        @pl.when(present)
        def _():
            bb = st_in[side, 0].astype(F32)
            ext_b[where, :] = bb
            ext_m[where, :] = time_step * st_in[side, 1].astype(F32)
            hh = h_in[side]
            ext_h[where, :] = hh
            ext_s0[where, :] = bb + hh

        @pl.when(jnp.logical_not(present))
        def _():
            for ref in (ext_h, ext_s0, ext_s1, ext_d):
                ref[where, :] = zeros
    fill(0, top, has_up)
    fill(1, low, has_down)
    wait_halo(2)

    def fill_e(side, where, present):
        @pl.when(present)
        def _():
            ext_e[where, :] = slide_rate * jnp.exp(-f_in[side].astype(F32))
    fill_e(0, top, has_up)
    fill_e(1, low, has_down)

    for m in range(2 * B):
        s1copy(m).wait_send()
    for q in range(B):
        s2copy(q).wait_send()
        if ks[q]:
            s3copy(q).wait_send()

    col = lax.broadcasted_iota(jnp.int32, (8, cols), 1)
    first_col, last_col = col == 0, col == cols - 1

    def before(v):
        return jnp.where(first_col, 0.0, pltpu.roll(v, 1, 1))

    def after(v):
        return jnp.where(last_col, 0.0, pltpu.roll(v, cols - 1, 1))

    row = lax.broadcasted_iota(jnp.int32, (8, cols), 0)
    first_row, last_row = row == 0, row == 7

    def above(ref, r, v):
        prev = ref[pl.ds(pl.multiple_of(r - 8, 8), 8), :]
        return pltpu.roll(jnp.where(last_row, prev, v), 1, 0)

    def below(ref, r, v):
        following = ref[pl.ds(pl.multiple_of(r + 8, 8), 8), :]
        return pltpu.roll(jnp.where(first_row, following, v), 7, 0)

    blocks = rows // 8
    lowest = jnp.where(has_up, 0, blocks)
    highest = jnp.where(has_down, 3 * blocks, 2 * blocks)
    total = 3 * rows
    margin = rows - 2 * STEPS

    for t in range(1, STEPS + 1):
        s_ref, s_new = (ext_s0, ext_s1) if t % 2 else (ext_s1, ext_s0)
        lo_h = margin + 2 * t
        lo_d = lo_h - 1

        def d_block(i, carry):
            r = PAD + i * 8
            here = pl.ds(pl.multiple_of(r, 8), 8)
            s = s_ref[here, :]
            gx = below(s_ref, r, s) - above(s_ref, r, s)
            gy = after(s) - before(s)
            h = ext_h[here, :]
            sq = h * h
            d = (0.25 * flow_rate) * (sq * sq * h) * (gx * gx + gy * gy) + sq * ext_e[here, :]
            ext_d[here, :] = jnp.minimum(d, diff_cap)
            return carry

        def h_block(i, carry):
            r = PAD + i * 8
            here = pl.ds(pl.multiple_of(r, 8), 8)
            s, d = s_ref[here, :], ext_d[here, :]
            div = (below(ext_d, r, d) + d) * (below(s_ref, r, s) - s)
            div += (above(ext_d, r, d) + d) * (above(s_ref, r, s) - s)
            div += (after(d) + d) * (after(s) - s)
            div += (before(d) + d) * (before(s) - s)
            h = jnp.maximum(ext_h[here, :] + ((0.5 * time_step) * div + ext_m[here, :]), 0.0)
            if t < STEPS:
                ext_h[here, :] = h
                s_new[here, :] = ext_b[here, :] + h
            else:
                final_ref[pl.ds(pl.multiple_of(i * 8 - rows, 8), 8), :] = h
            return carry

        lax.fori_loop(jnp.maximum(lowest, lo_d // 8), jnp.minimum(highest, -(-(total - lo_d) // 8)), d_block, 0)
        lax.fori_loop(jnp.maximum(lowest, lo_h // 8), jnp.minimum(highest, -(-(total - lo_h) // 8)), h_block, 0)


def per_device(n, mode_fields, coeff, eigen, map_friction, bed, smb, thickness):
    rows, cols = map_friction.shape
    mode_dev = mode_fields.shape[0]
    B = n // 4
    modes = coeff.shape[0]
    vmem = pl.BlockSpec(memory_space=pltpu.VMEM)
    strip = (rows, cols)
    ext = (3 * rows + 2 * PAD, cols)
    bf = jnp.bfloat16
    dma = pltpu.SemaphoreType.DMA
    return pl.pallas_call(
        functools.partial(kernel, n),
        out_shape=(jax.ShapeDtypeStruct(strip, F32),) * 2,
        in_specs=[vmem] * 6 + [pl.BlockSpec(memory_space=pl.ANY)],
        out_specs=(vmem, vmem),
        scratch_shapes=[
            pltpu.VMEM((mode_dev, n * rows, cols), bf),
            pltpu.VMEM((2 * B,) + strip, F32),
            pltpu.VMEM((2 * B,) + strip, F32),
            pltpu.VMEM((2 * B,) + strip, F32),
            pltpu.VMEM((B,) + strip, WIRE),
            pltpu.VMEM((B,) + strip, WIRE),
            pltpu.VMEM((B,) + strip, WIRE),
            pltpu.VMEM((B,) + strip, WIRE),
            pltpu.VMEM(strip, F32),
            pltpu.VMEM((2,) + strip, bf),
            pltpu.VMEM((2, 2) + strip, bf),
            pltpu.VMEM((2,) + strip, F32),
            pltpu.VMEM(strip, bf),
            pltpu.VMEM((2,) + strip, bf),
        ] + [pltpu.VMEM(ext, F32)] * 7 + [
            dma((n,)), dma((2 * B,)), dma((2 * B,)), dma((B,)), dma((B,)), dma((B,)), dma((B,)), dma((6,)), dma((6,)),
        ],
        compiler_params=pltpu.CompilerParams(collective_id=0, has_side_effects=True, vmem_limit_bytes=60 * 2**20),
        name="posterior_ice",
    )(coeff.reshape(1, modes), eigen.reshape(1, modes), map_friction, bed, smb, thickness, mode_fields)


def solution(mesh):
    n = mesh.shape["modes"]
    return jax.shard_map(
        functools.partial(per_device, n),
        mesh=mesh,
        in_specs=(
            P(("groups", "modes"), None, None),
            P("groups"),
            P("groups"),
            P(("groups", "modes"), None),
            P(("groups", "modes"), None),
            P(("groups", "modes"), None),
            P(("groups", "modes"), None),
        ),
        out_specs=(P(("groups", "modes"), None), P(("groups", "modes"), None)),
        check_vma=False,
    )
```

time: 118 us -> 39.5 us (0.33)
  waiting for transfers between devices: 62.1 us -> 0 us
  Pallas kernels: 0 us -> 35.5 us
  other arithmetic: 14.2 us -> 0 us
  between operations: 14.4 us -> 0.64 us
  starting transfers between devices: 13.5 us -> 0 us
  matrix products: 9.37 us -> 0 us
    reduce_scatter x1 -> x0, waiting for transfers between devices: 54.2 us -> none  [per_device(): lax.psum_scatter(jnp.einsum('k,kxy->xy', local_w, mode_fields, preferred_...]
    pallas_call x0 -> x1, Pallas kernels: none -> 35.5 us  [per_device(): pl.pallas_call(functools.partial(kernel, n), out_shape=(jax.ShapeDtypeStr...]
    ppermute x4 -> x0, starting transfers between devices: 13.5 us -> none  [the longest x2 9.45 us: padded(): before = lax.ppermute(last, axis, up)]
    dot_general x1 -> x0, matrix products: 9.37 us -> none  [per_device(): jnp.einsum('k,kxy->xy', local_w, mode_fields, preferred_element_type=jnp....]
    ppermute x4 -> x0, waiting for transfers between devices: 7.84 us -> none  [the longest x2 5.3 us: padded(): after = lax.ppermute(leading, axis, down)]
    min x8 -> x0, other arithmetic: 5.76 us -> none  [advance(): diff = jnp.minimum(diff + slide_rate * squared * jnp.exp(-fcent), diff_cap)]
    select_n x7 -> x0, other arithmetic: 5.59 us -> none  [march(): extended = jnp.where(inside[:, None], extended, 0.0)]
    unnamed x12 -> x2, local copies, waits for them, and re-layouts: 0.91 us -> 3.14 us
  transfers between devices with their start and end apart: 5 -> 0, of which waited for: 3 -> 0; matrix products, arithmetic and copies ran while one was open for 1% -> 0% of each run, Pallas kernels for 0% -> 0%
where the time goes in v1:
time: 39.5 us; the launch traced here: 39.3 us
  Pallas kernels  35.5 us (90%)
  local copies, waits for them, and re-layouts  3.14 us (8%)
  between operations  0.64 us (2%)
    pallas_call x1, Pallas kernels, per_device(): pl.pallas_call(functools.partial(kernel, n), out_shape=(jax.ShapeDtypeStr...  35.5 us
    unnamed x2, local copies, waits for them, and re-layouts  3.14 us

profile of v1, /device:TPU:5, one launch (start us, length us, event | category | flops | bytes accessed | tf_op | source)
XLA Modules:
  0.0 39.3 jit_solution(18387791080085578574)
XLA Ops:
  0.6 35.5 %posterior_ice.1 = (f32[16,2048]{1,0:T(8,128)}, f32[16,2048]{1,0:T(8,128)}) custom-call(f32[1,128]{1,0:T(1,128)} %bitcast.2, f32[1,128]{1,0:T(1,128)} %bitcast.3, f32[16,2048]{1,0:T(8,128)} %map_ref.1, f32[16,2048]{1,0:T(8,128)} %bed_ref.1, f32[16,2048]{1,0:T(8,128)} %smb_ref.1, f32[16,2048]{1,0:T(8,128)} %h0_ref.1, bf16[8,256,2048]{2,1,0:T(8,128)(2,1)} %fields_ref.1), custom_call_target="tpu_custom_call" | custom-call | tf_op jit(solution)/shard_map/posterior_ice/pallas_call | solution.py:316
  36.2 1.6 %copy.11 = f32[16,2048]{1,0:T(8,128)} copy(f32[16,2048]{1,0:T(8,128)} %get-tuple-element.4) | data formatting | bytes 262144
  37.7 1.6 %copy.12 = f32[16,2048]{1,0:T(8,128)} copy(f32[16,2048]{1,0:T(8,128)} %get-tuple-element.5) | data formatting | bytes 262144

commit v2 on v1

--- a/solution.py
+++ b/solution.py
@@ -16,16 +16,19 @@
 
 WIRE = jnp.bfloat16
 PAD = 8
+LANES = 128
+GROUP = 4
 F32 = jnp.float32
 
 
 def kernel(
     n,
-    coeff_ref, eigen_ref, map_ref, bed_ref, smb_ref, h0_ref, fields_ref,
-    logf_ref, final_ref,
+    coeff_hbm, eigen_hbm, map_hbm, bed_hbm, smb_hbm, h0_hbm, fields_ref,
+    logf_hbm, final_hbm,
+    coeff_ref, eigen_ref, map_ref, bed_ref, smb_ref, h0_ref, logf_ref, final_ref, in_sem, out_sem,
     mf, p1out, p1own, p1in, s2out, s2in, s3out, s3in, acc,
-    st_out, st_in, h_in, f_out, f_in,
-    ext_b, ext_e, ext_m, ext_h, ext_d, ext_s0, ext_s1,
+    st_out, st_in, f_out, f_in,
+    ext_b, ext_e, ext_m, ext_h, ext_d, ext_g, ext_s0, ext_s1,
     mf_sem, p1s, p1r, s2s, s2r, s3s, s3r, hs, hr,
 ):
     me = lax.axis_index("modes")
@@ -53,6 +56,12 @@
         rr = pl.ds(pl.multiple_of(dest_of(k, aa, cc) * rows, rows), rows)
         return pltpu.make_async_copy(fields_ref.at[:, rr, :], mf.at[:, pl.ds(i * rows, rows), :], mf_sem.at[i])
 
+    hbm = (bed_hbm, smb_hbm, h0_hbm, coeff_hbm, eigen_hbm, map_hbm)
+    own = (bed_ref, smb_ref, h0_ref, coeff_ref, eigen_ref, map_ref)
+    takes = [pltpu.make_async_copy(x, y, in_sem.at[i]) for i, (x, y) in enumerate(zip(hbm, own))]
+    gives = [pltpu.make_async_copy(x, y, out_sem.at[i]) for i, (x, y) in enumerate(((logf_ref, logf_hbm), (final_ref, final_hbm)))]
+    for take in takes:
+        take.start()
     for i in range(n):
         load(i).start()
 
@@ -67,6 +76,8 @@
     for peer in [left, right, core_peer, y_peer] + [z_peer(k) for k in range(1, B)]:
         pl.semaphore_signal(barrier, inc=1, device_id={"modes": peer}, device_id_type=pl.DeviceIdType.MESH)
 
+    for take in takes:
+        take.wait()
     w = coeff_ref[...] / jnp.sqrt(1.0 + eigen_ref[...])
     w = w.astype(jnp.bfloat16).astype(F32)
     lane = lax.broadcasted_iota(jnp.int32, w.shape, 1)
@@ -76,6 +87,7 @@
         ws.append(jnp.sum(picked, axis=1, keepdims=True))
     st_out[0] = bed_ref[...].astype(jnp.bfloat16)
     st_out[1] = smb_ref[...].astype(jnp.bfloat16)
+    st_out[2] = h0_ref[...].astype(jnp.bfloat16)
 
     pl.semaphore_wait(barrier, 4 + B - 1)
 
@@ -85,8 +97,8 @@
             device_id={"modes": peer}, device_id_type=pl.DeviceIdType.MESH)
 
     def halo(kind, side):
-        src = (st_out, h0_ref, f_out)[kind]
-        dst = (st_in, h_in, f_in)[kind]
+        src = (st_out, f_out)[kind]
+        dst = (st_in, f_in)[kind]
         peer = right if side == 0 else left
         at = kind * 2 + side
         return remote(src, dst.at[side], hs.at[at], hr.at[at], peer)
@@ -113,7 +125,6 @@
             halo(kind, 1).wait_send()
             halo(kind, 0).wait_recv()
 
-    start_halo(1)
     start_halo(0)
 
     CT = min(512, cols)
@@ -192,44 +203,60 @@
         logf_ref[:, cs] = tot
         f_out[:, cs] = tot.astype(jnp.bfloat16)
     col_loop(finish)
-    start_halo(2)
-
+    start_halo(1)
+    gives[0].start()
+
+    tiles = cols // LANES
     top, mid, low = pl.ds(PAD, rows), pl.ds(PAD + rows, rows), pl.ds(PAD + 2 * rows, rows)
-    zeros = jnp.zeros((rows, cols), F32)
-    for ref in (ext_s0, ext_s1, ext_d, ext_h):
-        ref[pl.ds(0, PAD), :] = jnp.zeros((PAD, cols), F32)
-        ref[pl.ds(PAD + 3 * rows, PAD), :] = jnp.zeros((PAD, cols), F32)
-
-    ext_b[mid, :] = bed_ref[...]
-    ext_m[mid, :] = time_step * smb_ref[...]
-    ext_h[mid, :] = h0_ref[...]
-    ext_s0[mid, :] = bed_ref[...] + h0_ref[...]
-    ext_e[mid, :] = slide_rate * jnp.exp(-logf_ref[...])
+    whole = 3 * rows + 2 * PAD
+
+    def clear(ref, where, size):
+        for j in range(tiles):
+            ref[j + 1, where, :] = jnp.zeros((size, LANES), F32)
+
+    for ref in (ext_s0, ext_s1, ext_d):
+        clear(ref, pl.ds(0, PAD), PAD)
+        clear(ref, pl.ds(PAD + 3 * rows, PAD), PAD)
+        for j in (0, tiles + 1):
+            ref[j] = jnp.zeros((whole, LANES), F32)
+    ext_g[0] = jnp.zeros((whole, LANES), F32)
+
+    def lanes(j):
+        return slice(j * LANES, (j + 1) * LANES)
+
+    for j in range(tiles):
+        bb, hh = bed_ref[:, lanes(j)], h0_ref[:, lanes(j)]
+        ext_b[j + 1, mid, :] = bb
+        ext_m[j + 1, mid, :] = time_step * smb_ref[:, lanes(j)]
+        ext_h[j + 1, mid, :] = hh
+        ext_s0[j + 1, mid, :] = bb + hh
+        ext_e[j + 1, mid, :] = slide_rate * jnp.exp(-logf_ref[:, lanes(j)])
     wait_halo(0)
-    wait_halo(1)
 
     def fill(side, where, present):
         @pl.when(present)
         def _():
-            bb = st_in[side, 0].astype(F32)
-            ext_b[where, :] = bb
-            ext_m[where, :] = time_step * st_in[side, 1].astype(F32)
-            hh = h_in[side]
-            ext_h[where, :] = hh
-            ext_s0[where, :] = bb + hh
+            for j in range(tiles):
+                bb = st_in[side, 0, :, lanes(j)].astype(F32)
+                hh = st_in[side, 2, :, lanes(j)].astype(F32)
+                ext_b[j + 1, where, :] = bb
+                ext_m[j + 1, where, :] = time_step * st_in[side, 1, :, lanes(j)].astype(F32)
+                ext_h[j + 1, where, :] = hh
+                ext_s0[j + 1, where, :] = bb + hh
 
         @pl.when(jnp.logical_not(present))
         def _():
-            for ref in (ext_h, ext_s0, ext_s1, ext_d):
-                ref[where, :] = zeros
+            for ref in (ext_s0, ext_s1, ext_d):
+                clear(ref, where, rows)
     fill(0, top, has_up)
     fill(1, low, has_down)
-    wait_halo(2)
+    wait_halo(1)
 
     def fill_e(side, where, present):
         @pl.when(present)
         def _():
-            ext_e[where, :] = slide_rate * jnp.exp(-f_in[side].astype(F32))
+            for j in range(tiles):
+                ext_e[j + 1, where, :] = slide_rate * jnp.exp(-f_in[side, :, lanes(j)].astype(F32))
     fill_e(0, top, has_up)
     fill_e(1, low, has_down)
 
@@ -240,67 +267,68 @@
         if ks[q]:
             s3copy(q).wait_send()
 
-    col = lax.broadcasted_iota(jnp.int32, (8, cols), 1)
-    first_col, last_col = col == 0, col == cols - 1
-
-    def before(v):
-        return jnp.where(first_col, 0.0, pltpu.roll(v, 1, 1))
-
-    def after(v):
-        return jnp.where(last_col, 0.0, pltpu.roll(v, cols - 1, 1))
-
-    row = lax.broadcasted_iota(jnp.int32, (8, cols), 0)
-    first_row, last_row = row == 0, row == 7
-
-    def above(ref, r, v):
-        prev = ref[pl.ds(pl.multiple_of(r - 8, 8), 8), :]
-        return pltpu.roll(jnp.where(last_row, prev, v), 1, 0)
-
-    def below(ref, r, v):
-        following = ref[pl.ds(pl.multiple_of(r + 8, 8), 8), :]
-        return pltpu.roll(jnp.where(first_row, following, v), 7, 0)
-
-    blocks = rows // 8
-    lowest = jnp.where(has_up, 0, blocks)
-    highest = jnp.where(has_down, 3 * blocks, 2 * blocks)
-    total = 3 * rows
     margin = rows - 2 * STEPS
+
+    def sweep(first, last, body):
+        for lo, hi, present in ((0, rows, has_up), (rows, 2 * rows, None), (2 * rows, 3 * rows, has_down)):
+            lo, hi = max(lo, first // 8 * 8), min(hi, -(-last // 8) * 8)
+            if lo >= hi:
+                continue
+            if present is None:
+                body(PAD + lo, hi - lo)
+            else:
+                pl.when(present)(functools.partial(body, PAD + lo, hi - lo))
 
     for t in range(1, STEPS + 1):
         s_ref, s_new = (ext_s0, ext_s1) if t % 2 else (ext_s1, ext_s0)
         lo_h = margin + 2 * t
-        lo_d = lo_h - 1
-
-        def d_block(i, carry):
-            r = PAD + i * 8
-            here = pl.ds(pl.multiple_of(r, 8), 8)
-            s = s_ref[here, :]
-            gx = below(s_ref, r, s) - above(s_ref, r, s)
-            gy = after(s) - before(s)
-            h = ext_h[here, :]
-            sq = h * h
-            d = (0.25 * flow_rate) * (sq * sq * h) * (gx * gx + gy * gy) + sq * ext_e[here, :]
-            ext_d[here, :] = jnp.minimum(d, diff_cap)
-            return carry
-
-        def h_block(i, carry):
-            r = PAD + i * 8
-            here = pl.ds(pl.multiple_of(r, 8), 8)
-            s, d = s_ref[here, :], ext_d[here, :]
-            div = (below(ext_d, r, d) + d) * (below(s_ref, r, s) - s)
-            div += (above(ext_d, r, d) + d) * (above(s_ref, r, s) - s)
-            div += (after(d) + d) * (after(s) - s)
-            div += (before(d) + d) * (before(s) - s)
-            h = jnp.maximum(ext_h[here, :] + ((0.5 * time_step) * div + ext_m[here, :]), 0.0)
-            if t < STEPS:
-                ext_h[here, :] = h
-                s_new[here, :] = ext_b[here, :] + h
-            else:
-                final_ref[pl.ds(pl.multiple_of(i * 8 - rows, 8), 8), :] = h
-            return carry
-
-        lax.fori_loop(jnp.maximum(lowest, lo_d // 8), jnp.minimum(highest, -(-(total - lo_d) // 8)), d_block, 0)
-        lax.fori_loop(jnp.maximum(lowest, lo_h // 8), jnp.minimum(highest, -(-(total - lo_h) // 8)), h_block, 0)
+
+        lane = lax.broadcasted_iota(jnp.int32, (1, 8, LANES), 2)
+        first_lane, last_lane = lane == 0, lane == LANES - 1
+
+        def d_rows(r, size):
+            for at in range(r, r + size, 8):
+                here, up, down = (slice(at + o, at + o + 8) for o in (0, -1, 1))
+                for j in range(1, tiles + 1, GROUP):
+                    now, later, sooner = (slice(j + o, j + o + GROUP) for o in (0, 1, -1))
+                    s = s_ref[now, here, :]
+                    right = pltpu.roll(jnp.where(first_lane, s_ref[later, here, :], s), LANES - 1, 2)
+                    left_ = pltpu.roll(jnp.where(last_lane, s_ref[sooner, here, :], s), 1, 2)
+                    gx = s_ref[now, down, :] - s_ref[now, up, :]
+                    gy = right - left_
+                    h = ext_h[now, here, :]
+                    sq = h * h
+                    d = sq * ((0.25 * flow_rate) * (sq * h) * (gx * gx + gy * gy) + ext_e[now, here, :])
+                    ext_d[now, here, :] = jnp.minimum(d, diff_cap)
+                    ext_g[now, here, :] = right - s
+
+        def h_rows(r, size):
+            for at in range(r, r + size, 8):
+                here, up, down = (slice(at + o, at + o + 8) for o in (0, -1, 1))
+                edge = pltpu.roll(ext_d[1:2, here, :] * s_ref[1:2, here, :], LANES - 1, 2)
+                for j in range(1, tiles + 1, GROUP):
+                    now, later = (slice(j + o, j + o + GROUP) for o in (0, 1))
+                    s, d = s_ref[now, here, :], ext_d[now, here, :]
+                    right = pltpu.roll(jnp.where(first_lane, ext_d[later, here, :], d), LANES - 1, 2)
+                    flux = (right + d) * ext_g[now, here, :]
+                    sooner = jnp.concatenate([edge, flux[:-1]], axis=0)
+                    edge = flux[-1:]
+                    div = (ext_d[now, down, :] + d) * (s_ref[now, down, :] - s)
+                    div += (ext_d[now, up, :] + d) * (s_ref[now, up, :] - s)
+                    div += flux - pltpu.roll(jnp.where(last_lane, sooner, flux), 1, 2)
+                    h = jnp.maximum(ext_h[now, here, :] + ((0.5 * time_step) * div + ext_m[now, here, :]), 0.0)
+                    ext_h[now, here, :] = h
+                    if t < STEPS:
+                        s_new[now, here, :] = ext_b[now, here, :] + h
+
+        sweep(lo_h - 1, 3 * rows - lo_h + 1, d_rows)
+        sweep(lo_h, 3 * rows - lo_h, h_rows)
+
+    for j in range(tiles):
+        final_ref[:, lanes(j)] = ext_h[j + 1, mid, :]
+    gives[1].start()
+    gives[0].wait()
+    gives[1].wait()
 
 
 def per_device(n, mode_fields, coeff, eigen, map_friction, bed, smb, thickness):
@@ -308,17 +336,22 @@
     mode_dev = mode_fields.shape[0]
     B = n // 4
     modes = coeff.shape[0]
-    vmem = pl.BlockSpec(memory_space=pltpu.VMEM)
+    anywhere = pl.BlockSpec(memory_space=pl.ANY)
     strip = (rows, cols)
-    ext = (3 * rows + 2 * PAD, cols)
+    ext = (cols // LANES + 2, 3 * rows + 2 * PAD, LANES)
     bf = jnp.bfloat16
     dma = pltpu.SemaphoreType.DMA
     return pl.pallas_call(
         functools.partial(kernel, n),
         out_shape=(jax.ShapeDtypeStruct(strip, F32),) * 2,
-        in_specs=[vmem] * 6 + [pl.BlockSpec(memory_space=pl.ANY)],
-        out_specs=(vmem, vmem),
+        in_specs=[anywhere] * 7,
+        out_specs=(anywhere, anywhere),
         scratch_shapes=[
+            pltpu.VMEM((1, modes), F32),
+            pltpu.VMEM((1, modes), F32),
+        ] + [pltpu.VMEM(strip, F32)] * 6 + [
+            dma((6,)),
+            dma((2,)),
             pltpu.VMEM((mode_dev, n * rows, cols), bf),
             pltpu.VMEM((2 * B,) + strip, F32),
             pltpu.VMEM((2 * B,) + strip, F32),
@@ -328,13 +361,12 @@
             pltpu.VMEM((B,) + strip, WIRE),
             pltpu.VMEM((B,) + strip, WIRE),
             pltpu.VMEM(strip, F32),
-            pltpu.VMEM((2,) + strip, bf),
-            pltpu.VMEM((2, 2) + strip, bf),
-            pltpu.VMEM((2,) + strip, F32),
+            pltpu.VMEM((3,) + strip, bf),
+            pltpu.VMEM((2, 3) + strip, bf),
             pltpu.VMEM(strip, bf),
             pltpu.VMEM((2,) + strip, bf),
-        ] + [pltpu.VMEM(ext, F32)] * 7 + [
-            dma((n,)), dma((2 * B,)), dma((2 * B,)), dma((B,)), dma((B,)), dma((B,)), dma((B,)), dma((6,)), dma((6,)),
+        ] + [pltpu.VMEM(ext, F32)] * 8 + [
+            dma((n,)), dma((2 * B,)), dma((2 * B,)), dma((B,)), dma((B,)), dma((B,)), dma((B,)), dma((4,)), dma((4,)),
         ],
         compiler_params=pltpu.CompilerParams(collective_id=0, has_side_effects=True, vmem_limit_bytes=60 * 2**20),
         name="posterior_ice",

time: 39.5 us -> 37.4 us (0.947)
  Pallas kernels: 35.5 us -> 33.5 us
    pallas_call x1, Pallas kernels: 35.5 us -> 33.5 us  [per_device(): pl.pallas_call(functools.partial(kernel, n), out_shape=(jax.ShapeDtypeStr...]
where the time goes in v2:
time: 37.4 us; the launch traced here: 37.3 us
  Pallas kernels  33.5 us (90%)
  local copies, waits for them, and re-layouts  3.14 us (8%)
  between operations  0.64 us (2%)
    pallas_call x1, Pallas kernels, per_device(): pl.pallas_call(functools.partial(kernel, n), out_shape=(jax.ShapeDtypeStr...  33.5 us
    unnamed x2, local copies, waits for them, and re-layouts  3.14 us

profile of v2, /device:TPU:5, one launch (start us, length us, event | category | flops | bytes accessed | tf_op | source)
XLA Modules:
  0.0 37.3 jit_solution(14387812408027484505)
XLA Ops:
  0.6 33.5 %posterior_ice.1 = (f32[16,2048]{1,0:T(8,128)}, f32[16,2048]{1,0:T(8,128)}) custom-call(f32[1,128]{1,0:T(1,128)} %bitcast.2, f32[1,128]{1,0:T(1,128)} %bitcast.3, f32[16,2048]{1,0:T(8,128)} %map_hbm.1, f32[16,2048]{1,0:T(8,128)} %bed_hbm.1, f32[16,2048]{1,0:T(8,128)} %smb_hbm.1, f32[16,2048]{1,0:T(8,128)} %h0_hbm.1, bf16[8,256,2048]{2,1,0:T(8,128)(2,1)} %fields_ref.1), custom_call_target="tpu_custom_call" | custom-call | tf_op jit(solution)/shard_map/posterior_ice/pallas_call | solution.py:344
  34.1 1.6 %copy.11 = f32[16,2048]{1,0:T(8,128)} copy(f32[16,2048]{1,0:T(8,128)} %get-tuple-element.4) | data formatting | bytes 262144
  35.7 1.6 %copy.12 = f32[16,2048]{1,0:T(8,128)} copy(f32[16,2048]{1,0:T(8,128)} %get-tuple-element.5) | data formatting | bytes 262144

commit v3 on v2

--- a/solution.py
+++ b/solution.py
@@ -125,7 +125,6 @@
             halo(kind, 1).wait_send()
             halo(kind, 0).wait_recv()
 
-    start_halo(0)
 
     CT = min(512, cols)
 
@@ -193,6 +192,7 @@
         stage1(B + q)
     for q in range(B):
         stage3(q)
+    start_halo(0)
     for q in range(B - 1):
         s3copy(q).wait_recv()
 

time: 37.4 us -> 35.4 us (0.947)
  Pallas kernels: 33.5 us -> 31.5 us
    pallas_call x1, Pallas kernels: 33.5 us -> 31.5 us  [per_device(): pl.pallas_call(functools.partial(kernel, n), out_shape=(jax.ShapeDtypeStr...]
where the time goes in v3:
time: 35.4 us; the launch traced here: 35.3 us
  Pallas kernels  31.5 us (89%)
  local copies, waits for them, and re-layouts  3.14 us (9%)
  between operations  0.64 us (2%)
    pallas_call x1, Pallas kernels, per_device(): pl.pallas_call(functools.partial(kernel, n), out_shape=(jax.ShapeDtypeStr...  31.5 us
    unnamed x2, local copies, waits for them, and re-layouts  3.14 us

profile of v3, /device:TPU:5, one launch (start us, length us, event | category | flops | bytes accessed | tf_op | source)
XLA Modules:
  0.0 35.3 jit_solution(6599262630691271704)
XLA Ops:
  0.6 31.5 %posterior_ice.1 = (f32[16,2048]{1,0:T(8,128)}, f32[16,2048]{1,0:T(8,128)}) custom-call(f32[1,128]{1,0:T(1,128)} %bitcast.2, f32[1,128]{1,0:T(1,128)} %bitcast.3, f32[16,2048]{1,0:T(8,128)} %map_hbm.1, f32[16,2048]{1,0:T(8,128)} %bed_hbm.1, f32[16,2048]{1,0:T(8,128)} %smb_hbm.1, f32[16,2048]{1,0:T(8,128)} %h0_hbm.1, bf16[8,256,2048]{2,1,0:T(8,128)(2,1)} %fields_ref.1), custom_call_target="tpu_custom_call" | custom-call | tf_op jit(solution)/shard_map/posterior_ice/pallas_call | solution.py:344
  32.1 1.6 %copy.11 = f32[16,2048]{1,0:T(8,128)} copy(f32[16,2048]{1,0:T(8,128)} %get-tuple-element.4) | data formatting | bytes 262144
  33.7 1.6 %copy.12 = f32[16,2048]{1,0:T(8,128)} copy(f32[16,2048]{1,0:T(8,128)} %get-tuple-element.5) | data formatting | bytes 262144
